TPU v7x, 32 devices: a whole 2x2x4 slice. The times are simulated.
32 devices in a mesh: seq: 8 (over z, y), head: 4 (over x, core).
Axes of the slice: x: 2, y: 2, z: 4, core: 2. Of those that a mesh axis runs over, the one named last changes fastest.
Arguments:
- queries: bfloat16 [4096, 4096], P('seq', 'head'), may hold values from -6 to 6
- keys: bfloat16 [4096, 4096], P('seq', 'head'), may hold values from -6 to 6
- values: bfloat16 [4096, 4096], P('seq', 'head'), may hold values from -6 to 6
- level_weights: float32 [5, 32, 4096], P(None, 'head', 'seq'), may hold values from 0.1 to 3, as said below
- norm_gain: float32 [4096], P('head'), may hold values from 0.25 to 1.75
Outputs:
- mixed: bfloat16 [4096, 4096], P('seq', 'head')
Inputs may be any that keep to these rules, and one draw needn't show every extreme that they name: `level_weights`: positive level weights.
All inputs are finite; a program needn't handle non-finite values.
Results may differ from a plain program's by a relative error of at most 0.0049.
Values may be sent and summed in bfloat16 or wider, within the bound.
No kernel may reach another device: no remote copies, remote signals or barrier semaphores. Data moves between devices by JAX's collectives and lax.ppermute only.
A program may use at most 64 MiB of HBM per device.

v0:
```python
import jax
import jax.numpy as jnp
from jax import lax
from jax.sharding import PartitionSpec as P

HEAD_DIM = 128
STRETCH = 256
D = 4096
EPSILON = 1e-06


def swapped(block, axis, stride):
    count = lax.axis_size(axis)
    route = []
    for low in range(count):
        high = low | 1 << stride
        if high != low and high < count:
            route += [(low, high), (high, low)]
    return lax.ppermute(block, axis, route)


def shifted(block, axis, distance):
    devices = range(lax.axis_size(axis))
    route = [(i - distance, i) for i in devices if i - distance in devices]
    return lax.ppermute(block, axis, route)


def local(queries, keys, values, level_weights, norm_gain):
    tok_rows = queries.shape[0]
    heads_here = queries.shape[1] // HEAD_DIM
    stretch_count = tok_rows // STRETCH
    block_shape = (stretch_count, STRETCH, heads_here, HEAD_DIM)
    query_block_list = queries.reshape(block_shape)
    key_blocks = keys.reshape(block_shape)
    value_blocks = values.reshape(block_shape)
    level_total = level_weights.shape[0]
    weights_here = level_weights.reshape(level_total, heads_here, stretch_count, STRETCH).transpose(
        0, 2, 3, 1
    )
    states = jnp.einsum(
        "cthk,cthv->chkv", key_blocks, value_blocks, preferred_element_type=jnp.float32
    )
    scores = jnp.einsum(
        "cthk,cshk->chts", query_block_list, key_blocks, preferred_element_type=jnp.float32
    )
    causal = lax.broadcasted_iota(jnp.int32, (STRETCH, STRETCH), 0) >= lax.broadcasted_iota(
        jnp.int32, (STRETCH, STRETCH), 1
    )
    attn_probs = jnp.where(causal[None, None], scores, 0.0).astype(jnp.bfloat16)
    intra_out = jnp.einsum(
        "chts,cshv->cthv", attn_probs, value_blocks, preferred_element_type=jnp.float32
    )
    combined = weights_here[0][..., None] * intra_out
    running = states
    local_bits = stretch_count.bit_length() - 1
    level_bit = 0
    groups = running.shape[0] // 2
    block_span = 2**level_bit
    halves = running.reshape(groups, 2, heads_here, HEAD_DIM, HEAD_DIM)
    leftward_sum = halves[:, 0].astype(jnp.bfloat16)
    rightward_queries = query_block_list.reshape(
        groups, 2, block_span * STRETCH, heads_here, HEAD_DIM
    )[:, 1]
    state_readout = jnp.einsum(
        "nthk,nhkv->nthv", rightward_queries, leftward_sum, preferred_element_type=jnp.float32
    )
    level_weight = weights_here[1 + level_bit].reshape(groups, 2, block_span * STRETCH, heads_here)[
        :, 1
    ]
    contrib = level_weight[..., None] * state_readout
    padded = jnp.stack([jnp.zeros_like(contrib), contrib], axis=1)
    combined = combined + padded.reshape(stretch_count, STRETCH, heads_here, HEAD_DIM)
    running = halves[:, 0] + halves[:, 1]
    device_sum = running[0]
    seq_count = lax.axis_size("seq")
    seq_bits = seq_count.bit_length() - 1
    position = lax.axis_index("seq")
    crossing_state_list = []
    for level_bit in range(seq_bits - 1):
        partner = swapped(device_sum, "seq", level_bit)
        is_right = position >> level_bit & 1 == 1
        crossing_state_list.append(
            jnp.where(is_right, partner, jnp.zeros_like(partner)).astype(jnp.bfloat16)
        )
        device_sum = device_sum + partner
    last_partner = shifted(device_sum.astype(jnp.bfloat16), "seq", seq_count // 2)
    crossing_state_list.append(last_partner)
    for number, state_per_level in enumerate(crossing_state_list):
        state_readout = jnp.einsum(
            "lwnx,nxq->lwnq", query_block_list, state_per_level, preferred_element_type=jnp.float32
        )
        combined = combined + weights_here[1 + local_bits + number][..., None] * state_readout
    squares = jnp.sum(combined * combined, axis=(2, 3)).reshape(tok_rows)
    total_squares = lax.psum(squares, "head")
    inverse_rms = lax.rsqrt(total_squares / D + EPSILON)
    flat_out = combined.reshape(tok_rows, heads_here * HEAD_DIM)
    mixed_out = flat_out * inverse_rms[:, None] * norm_gain[None, :]
    return mixed_out.astype(jnp.bfloat16)


def solution(mesh):
    return jax.shard_map(
        local,
        mesh=mesh,
        in_specs=(
            P("seq", "head"),
            P("seq", "head"),
            P("seq", "head"),
            P(None, "head", "seq"),
            P("head"),
        ),
        out_specs=P("seq", "head"),
        check_vma=False,
    )
```

profile of v0, /device:TPU:24, one launch (start us, length us, event | category | flops | bytes accessed | tf_op | source)
XLA Modules:
  0.0 59.7 jit_solution(3533077832521115567)
XLA Ops:
  0.0 0.0 copy-start.3
  0.0 1.6 %copy.53 = bf16[64,8,8,128]{3,2,1,0:T(8,128)(2,1)S(1)} copy(bf16[64,8,8,128]{3,1,2,0:T(8,128)(2,1)} %bitcast.103) | data formatting | bytes 2097152
  1.6 0.7 %copy.20 = bf16[2,256,8,128]{1,3,2,0:T(8,128)(2,1)S(1)} copy(bf16[2,256,8,128]{3,2,1,0:T(8,128)(2,1)S(1)} %bitcast.102) | data formatting | bytes 2097152 | tf_op jit(solution)/shard_map/reshape | solution.py:34
  2.3 0.0 copy-start
  2.3 0.0 copy-done.3
  2.3 0.3 copy.54
  2.6 0.0 copy-start.1
  2.6 0.0 copy-start.5
  2.6 0.0 copy-start.4
  2.6 0.4 convolution_bitcast_fusion.1
  3.0 0.2 copy-done
  3.2 0.8 %fusion.17 = f32[8,128,128]{2,1,0:T(8,128)} fusion(f32[1,2,8,128,128]{4,3,2,1,0:T(8,128)S(1)} %convolution_bitcast_fusion.1), kind=kLoop, calls=%fused_computation.27 | loop fusion | flops 131072 | bytes 1572864 | tf_op jit(solution)/shard_map/add | solution.py:73
  4.1 0.0 copy-done.1
  4.1 1.5 %collective-permute-start = (f32[8,128,128]{2,1,0:T(8,128)}, f32[8,128,128]{2,1,0:T(8,128)}, u32[]{:S(2)}, u32[]{:S(2)}) collective-permute-start(f32[8,128,128]{2,1,0:T(8,128)} %fusion.17), channel_id=1, source_target_pairs={{0,4},{4,0},{8,12},{12,8},{16,20},{20,16},{24,28},{28,24},{1,5},{5... | collective-permute-start | bytes 1572872 | tf_op jit(solution)/shard_map/ppermute | solution.py:19
  5.7 0.0 copy-done.5
  5.7 0.0 copy-done.4
  5.7 0.3 copy.52
  6.0 0.3 fusion.7
  6.4 4.2 %fusion.5 = f32[2,8,256,128]{2,3,1,0:T(8,128)} fusion(bf16[2,256,8,128]{1,3,2,0:T(8,128)(2,1)} %copy-done, pred[256,256]{1,0:T(8,128)(4,1)S(1)} %iota_compare_fusion, bf16[2,256,8,128]{3,2,1,0:T(8,128)(2,1)} %bitcast.101, bf16[2,256,8,128]{3,2,1,0:T(8,128)(2,1)S(1)} %bitcast.95), kind=kOutput, calls=%fused_computation.13 | convolution fusion | flops 538968064 | bytes 5308416 | tf_op jit(solution)/shard_map/chts,cshv->cthv/dot_general | solution.py:50
  10.6 7.5 %collective-permute-done = f32[8,128,128]{2,1,0:T(8,128)} collective-permute-done((f32[8,128,128]{2,1,0:T(8,128)}, f32[8,128,128]{2,1,0:T(8,128)}, u32[]{:S(2)}, u32[]{:S(2)}) %collective-permute-start) | collective-permute-done | bytes 524320 | tf_op jit(solution)/shard_map/ppermute | solution.py:19
  18.1 1.1 %fusion.34 = f32[8,128,128]{2,1,0:T(8,128)S(1)} fusion(f32[8,128,128]{2,1,0:T(8,128)} %collective-permute-done, f32[1,2,8,128,128]{4,3,2,1,0:T(8,128)S(1)} %convolution_bitcast_fusion.1), kind=kLoop, calls=%fused_computation.51 | loop fusion | flops 262144 | bytes 2097152 | tf_op jit(solution)/shard_map/add | solution.py:85
  19.2 0.5 collective-permute-start.1
  19.7 0.5 fusion.13
  20.2 11.8 %collective-permute-done.1 = f32[8,128,128]{2,1,0:T(8,128)S(1)} collective-permute-done((f32[8,128,128]{2,1,0:T(8,128)S(1)}, f32[8,128,128]{2,1,0:T(8,128)S(1)}, u32[]{:S(2)}, u32[]{:S(2)}) %collective-permute-start.1) | collective-permute-done | bytes 524320 | tf_op jit(solution)/shard_map/ppermute | solution.py:19
  32.1 0.1 add_convert_fusion
  32.1 0.0 copy-start.2
  32.1 1.4 %collective-permute-start.2 = (bf16[8,128,128]{2,1,0:T(8,128)(2,1)S(1)}, bf16[8,128,128]{2,1,0:T(8,128)(2,1)S(1)}, u32[]{:S(2)}, u32[]{:S(2)}) collective-permute-start(bf16[8,128,128]{2,1,0:T(8,128)(2,1)S(1)} %add_convert_fusion), channel_id=1, source_target_pairs={{0,16},{4,20},{8,24},{12,28},{1,17},{5,21},{9,25},{13,29},{2,18},{... | collective-permute-start | bytes 786440 | tf_op jit(solution)/shard_map/ppermute | solution.py:25
  33.6 0.5 fusion.11
  34.1 12.8 %collective-permute-done.2 = bf16[8,128,128]{2,1,0:T(8,128)(2,1)S(1)} collective-permute-done((bf16[8,128,128]{2,1,0:T(8,128)(2,1)S(1)}, bf16[8,128,128]{2,1,0:T(8,128)(2,1)S(1)}, u32[]{:S(2)}, u32[]{:S(2)}) %collective-permute-start.2) | collective-permute-done | bytes 262176 | tf_op jit(solution)/shard_map/ppermute | solution.py:25
  46.9 0.0 copy-done.2
  46.9 2.4 %multiply_reduce_fusion = (f32[2,256]{1,0:T(2,128)S(1)}, f32[2,256,8,128]{1,3,2,0:T(8,128)}) fusion(bf16[2,256,8,128]{3,2,1,0:T(8,128)(2,1)S(1)} %bitcast.98, bf16[8,128,128]{2,1,0:T(8,128)(2,1)S(1)} %collective-permute-done.2, f32[2,256,8]{1,2,0:T(8,128)S(1)} %get-tuple-element.6, f32[8,128,2,256]{3,1,0,2:T(8,128)S(1)} %fusion.11, ...), kind=kOutput, calls=%fused_computation.12 | convolution fusion | flops 139460096 | bytes 10815488 | tf_op jit(solution)/shard_map/lwnx,nxq->lwnq/dot_general | solution.py:89
  49.3 6.8 %psum.7 = f32[512]{0:T(512)S(1)} all-reduce(f32[512]{0:T(512)S(1)} %bitcast.109), channel_id=1, replica_groups=mesh['seq'=8,'head'=4] {'head'}, use_global_device_ids=true, to_apply=%region_1.2 | all-reduce | flops 512 | bytes 4096 | tf_op jit(solution)/shard_map/psum | solution.py:94
  56.1 0.0 copy-start.6
  56.1 2.1 %copy.33 = f32[2,256,8,128]{3,2,1,0:T(8,128)S(1)} copy(f32[2,256,8,128]{1,3,2,0:T(8,128)} %get-tuple-element.10) | data formatting | bytes 4194304 | tf_op jit(solution)/shard_map/add | solution.py:92
  58.3 0.0 copy-done.6
  58.3 1.4 %fusion.1 = bf16[512,1024]{1,0:T(8,128)(2,1)} fusion(f32[64,8,8,128]{3,2,1,0:T(8,128)S(1)} %bitcast.99, f32[1024]{0:T(1024)S(1)} %copy-done.6, f32[512]{0:T(512)S(1)} %add_rsqrt_fusion), kind=kLoop, calls=%fused_computation.3 | loop fusion | flops 1572864 | bytes 3151872 | tf_op jit(solution)/shard_map/convert_element_type | solution.py:98
  (6 shorter events, 0.1 us)
Async XLA Ops:
  0.0 2.3 %copy-start.3 = (bf16[512,1024]{1,0:T(8,128)(2,1)S(1)}, bf16[512,1024]{1,0:T(8,128)(2,1)}, u32[]{:S(2)}) copy-start(bf16[512,1024]{1,0:T(8,128)(2,1)} %param.7) | copy-start | bytes 3145732
  2.3 1.0 %copy-start = (bf16[2,256,8,128]{1,3,2,0:T(8,128)(2,1)}, bf16[2,256,8,128]{1,3,2,0:T(8,128)(2,1)S(1)}, u32[]{:S(2)}) copy-start(bf16[2,256,8,128]{1,3,2,0:T(8,128)(2,1)S(1)} %copy.20) | copy-start | bytes 3145732
  2.6 1.5 %copy-start.1 = (bf16[64,8,8,128]{3,2,1,0:T(8,128)(2,1)}, bf16[64,8,8,128]{3,2,1,0:T(8,128)(2,1)S(1)}, u32[]{:S(2)}) copy-start(bf16[64,8,8,128]{3,2,1,0:T(8,128)(2,1)S(1)} %copy.54) | copy-start | bytes 3145732
  2.6 3.1 %copy-start.5 = (f32[5,8,512]{2,1,0:T(8,128)S(1)}, f32[5,8,512]{2,1,0:T(8,128)}, u32[]{:S(2)}) copy-start(f32[5,8,512]{2,1,0:T(8,128)} %param.8) | copy-start | bytes 245764
  2.6 3.1 %copy-start.4 = (bf16[512,1024]{1,0:T(8,128)(2,1)S(1)}, bf16[512,1024]{1,0:T(8,128)(2,1)}, u32[]{:S(2)}) copy-start(bf16[512,1024]{1,0:T(8,128)(2,1)} %param.5) | copy-start | bytes 3145732
  4.1 14.0 %collective-permute-start = (f32[8,128,128]{2,1,0:T(8,128)}, f32[8,128,128]{2,1,0:T(8,128)}, u32[]{:S(2)}, u32[]{:S(2)}) collective-permute-start(f32[8,128,128]{2,1,0:T(8,128)} %fusion.17), channel_id=1, source_target_pairs={{0,4},{4,0},{8,12},{12,8},{16,20},{20,16},{24,28},{28,24},{1,5},{5... | collective-permute-start | bytes 1572872 | tf_op jit(solution)/shard_map/ppermute | solution.py:19
  19.2 12.9 %collective-permute-start.1 = (f32[8,128,128]{2,1,0:T(8,128)S(1)}, f32[8,128,128]{2,1,0:T(8,128)S(1)}, u32[]{:S(2)}, u32[]{:S(2)}) collective-permute-start(f32[8,128,128]{2,1,0:T(8,128)S(1)} %fusion.34), channel_id=1, source_target_pairs={{0,8},{8,0},{4,12},{12,4},{16,24},{24,16},{20,28},{28,20},{1,9},{9... | collective-permute-start | bytes 1572872 | tf_op jit(solution)/shard_map/ppermute | solution.py:19
  32.1 14.8 %copy-start.2 = (f32[2,8,256,128]{2,3,1,0:T(8,128)S(1)}, f32[2,8,256,128]{2,3,1,0:T(8,128)}, u32[]{:S(2)}) copy-start(f32[2,8,256,128]{2,3,1,0:T(8,128)} %fusion.5) | copy-start | bytes 6291460
  32.1 14.8 %collective-permute-start.2 = (bf16[8,128,128]{2,1,0:T(8,128)(2,1)S(1)}, bf16[8,128,128]{2,1,0:T(8,128)(2,1)S(1)}, u32[]{:S(2)}, u32[]{:S(2)}) collective-permute-start(bf16[8,128,128]{2,1,0:T(8,128)(2,1)S(1)} %add_convert_fusion), channel_id=1, source_target_pairs={{0,16},{4,20},{8,24},{12,28},{1,17},{5,21},{9,25},{13,29},{2,18},{... | collective-permute-start | bytes 786440 | tf_op jit(solution)/shard_map/ppermute | solution.py:25
  56.1 2.1 %copy-start.6 = (f32[1024]{0:T(1024)S(1)}, f32[1024]{0:T(1024)}, u32[]{:S(2)}) copy-start(f32[1024]{0:T(1024)} %param.9) | copy-start | bytes 12292
where the time goes:
time: 60 us; the launch traced here: 59.7 us
  waiting for transfers between devices  32.2 us (54%)
  matrix products  8.38 us (14%)
  blocking collectives  6.83 us (11%)
  local copies, waits for them, and re-layouts  5.2 us (9%)
  starting transfers between devices  3.46 us (6%)
  other arithmetic  3.45 us (6%)
    ppermute x2, waiting for transfers between devices, swapped(): return lax.ppermute(block, axis, route)  19.3 us
    ppermute x1, waiting for transfers between devices, shifted(): return lax.ppermute(block, axis, route)  12.8 us
    psum x1, blocking collectives, local(): total_squares = lax.psum(squares, 'head')  6.83 us
    dot_general x1, matrix products, local(): jnp.einsum('chts,cshv->cthv', attn_probs, value_blocks, preferred_element...  4.22 us
    dot_general x3, matrix products, local(): jnp.einsum('lwnx,nxq->lwnq', query_block_list, state_per_level, preferred...  3.39 us
    unnamed x18, local copies, waits for them, and re-layouts  2.36 us
    add x1, local copies, waits for them, and re-layouts, local(): combined + weights_here[1 + local_bits + number][..., None] * state_readout  2.12 us
    ppermute x2, starting transfers between devices, swapped(): return lax.ppermute(block, axis, route)  2.03 us
  transfers between devices with their start and end apart: 3, of which 3 were waited for; matrix products, arithmetic and copies ran while one was open for 10% of the time, Pallas kernels for 0%

commit v1 on v0

--- a/solution.py
+++ b/solution.py
@@ -91,7 +91,8 @@
         )
         combined = combined + weights_here[1 + local_bits + number][..., None] * state_readout
     squares = jnp.sum(combined * combined, axis=(2, 3)).reshape(tok_rows)
-    total_squares = lax.psum(squares, "head")
+    shards = lax.all_gather(squares, "head")
+    total_squares = jnp.sum(shards, axis=0)
     inverse_rms = lax.rsqrt(total_squares / D + EPSILON)
     flat_out = combined.reshape(tok_rows, heads_here * HEAD_DIM)
     mixed_out = flat_out * inverse_rms[:, None] * norm_gain[None, :]

time: 60 us -> 58.9 us (0.982)
  blocking collectives: 6.83 us -> 5.18 us
    psum x1 -> x0, blocking collectives: 6.83 us -> none  [local(): total_squares = lax.psum(squares, 'head')]
    all_gather x0 -> x1, blocking collectives: none -> 5.18 us  [local(): shards = lax.all_gather(squares, 'head')]
where the time goes in v1:
time: 58.9 us; the launch traced here: 58.1 us
  waiting for transfers between devices  32.2 us (55%)
  matrix products  8.38 us (14%)
  local copies, waits for them, and re-layouts  5.21 us (9%)
  blocking collectives  5.18 us (9%)
  other arithmetic  3.47 us (6%)
  starting transfers between devices  3.46 us (6%)
    ppermute x2, waiting for transfers between devices, swapped(): return lax.ppermute(block, axis, route)  19.3 us
    ppermute x1, waiting for transfers between devices, shifted(): return lax.ppermute(block, axis, route)  12.8 us
    all_gather x1, blocking collectives, local(): shards = lax.all_gather(squares, 'head')  5.18 us
    dot_general x1, matrix products, local(): jnp.einsum('chts,cshv->cthv', attn_probs, value_blocks, preferred_element...  4.22 us
    dot_general x3, matrix products, local(): jnp.einsum('lwnx,nxq->lwnq', query_block_list, state_per_level, preferred...  3.39 us
    unnamed x18, local copies, waits for them, and re-layouts  2.38 us
    add x1, local copies, waits for them, and re-layouts, local(): combined + weights_here[1 + local_bits + number][..., None] * state_readout  2.11 us
    ppermute x2, starting transfers between devices, swapped(): return lax.ppermute(block, axis, route)  2.03 us
  transfers between devices with their start and end apart: 3, of which 3 were waited for; matrix products, arithmetic and copies ran while one was open for 10% of the time, Pallas kernels for 0%

profile of v1, /device:TPU:24, one launch (start us, length us, event | category | flops | bytes accessed | tf_op | source)
XLA Modules:
  0.0 58.1 jit_solution(1504221375559089906)
XLA Ops:
  0.0 0.0 copy-start.3
  0.0 1.6 %copy.57 = bf16[64,8,8,128]{3,2,1,0:T(8,128)(2,1)S(1)} copy(bf16[64,8,8,128]{3,1,2,0:T(8,128)(2,1)} %bitcast.101) | data formatting | bytes 2097152
  1.6 0.7 %copy.37 = bf16[2,256,8,128]{1,3,2,0:T(8,128)(2,1)S(1)} copy(bf16[2,256,8,128]{3,2,1,0:T(8,128)(2,1)S(1)} %bitcast.100) | data formatting | bytes 2097152 | tf_op jit(solution)/shard_map/reshape | solution.py:34
  2.3 0.0 copy-start
  2.3 0.0 copy-done.3
  2.3 0.3 copy.58
  2.6 0.0 copy-start.1
  2.6 0.0 copy-start.5
  2.6 0.0 copy-start.4
  2.6 0.4 convolution_bitcast_fusion.1
  3.0 0.2 copy-done
  3.2 0.8 %fusion.17 = f32[8,128,128]{2,1,0:T(8,128)} fusion(f32[1,2,8,128,128]{4,3,2,1,0:T(8,128)S(1)} %convolution_bitcast_fusion.1), kind=kLoop, calls=%fused_computation.27 | loop fusion | flops 131072 | bytes 1572864 | tf_op jit(solution)/shard_map/add | solution.py:73
  4.1 0.0 copy-done.1
  4.1 1.5 %collective-permute-start = (f32[8,128,128]{2,1,0:T(8,128)}, f32[8,128,128]{2,1,0:T(8,128)}, u32[]{:S(2)}, u32[]{:S(2)}) collective-permute-start(f32[8,128,128]{2,1,0:T(8,128)} %fusion.17), channel_id=1, source_target_pairs={{0,4},{4,0},{8,12},{12,8},{16,20},{20,16},{24,28},{28,24},{1,5},{5... | collective-permute-start | bytes 1572872 | tf_op jit(solution)/shard_map/ppermute | solution.py:19
  5.7 0.0 copy-done.5
  5.7 0.0 copy-done.4
  5.7 0.3 copy.56
  6.0 0.3 fusion.7
  6.4 4.2 %fusion.5 = f32[2,8,256,128]{2,3,1,0:T(8,128)} fusion(bf16[2,256,8,128]{1,3,2,0:T(8,128)(2,1)} %copy-done, pred[256,256]{1,0:T(8,128)(4,1)S(1)} %iota_compare_fusion, bf16[2,256,8,128]{3,2,1,0:T(8,128)(2,1)} %bitcast.99, bf16[2,256,8,128]{3,2,1,0:T(8,128)(2,1)S(1)} %bitcast.93), kind=kOutput, calls=%fused_computation.13 | convolution fusion | flops 538968064 | bytes 5308416 | tf_op jit(solution)/shard_map/chts,cshv->cthv/dot_general | solution.py:50
  10.6 7.5 %collective-permute-done = f32[8,128,128]{2,1,0:T(8,128)} collective-permute-done((f32[8,128,128]{2,1,0:T(8,128)}, f32[8,128,128]{2,1,0:T(8,128)}, u32[]{:S(2)}, u32[]{:S(2)}) %collective-permute-start) | collective-permute-done | bytes 524320 | tf_op jit(solution)/shard_map/ppermute | solution.py:19
  18.1 1.1 %fusion.34 = f32[8,128,128]{2,1,0:T(8,128)S(1)} fusion(f32[8,128,128]{2,1,0:T(8,128)} %collective-permute-done, f32[1,2,8,128,128]{4,3,2,1,0:T(8,128)S(1)} %convolution_bitcast_fusion.1), kind=kLoop, calls=%fused_computation.51 | loop fusion | flops 262144 | bytes 2097152 | tf_op jit(solution)/shard_map/add | solution.py:85
  19.2 0.5 collective-permute-start.1
  19.7 0.5 fusion.13
  20.2 11.8 %collective-permute-done.1 = f32[8,128,128]{2,1,0:T(8,128)S(1)} collective-permute-done((f32[8,128,128]{2,1,0:T(8,128)S(1)}, f32[8,128,128]{2,1,0:T(8,128)S(1)}, u32[]{:S(2)}, u32[]{:S(2)}) %collective-permute-start.1) | collective-permute-done | bytes 524320 | tf_op jit(solution)/shard_map/ppermute | solution.py:19
  32.1 0.1 add_convert_fusion
  32.1 0.0 copy-start.2
  32.1 1.4 %collective-permute-start.2 = (bf16[8,128,128]{2,1,0:T(8,128)(2,1)S(1)}, bf16[8,128,128]{2,1,0:T(8,128)(2,1)S(1)}, u32[]{:S(2)}, u32[]{:S(2)}) collective-permute-start(bf16[8,128,128]{2,1,0:T(8,128)(2,1)S(1)} %add_convert_fusion), channel_id=1, source_target_pairs={{0,16},{4,20},{8,24},{12,28},{1,17},{5,21},{9,25},{13,29},{2,18},{... | collective-permute-start | bytes 786440 | tf_op jit(solution)/shard_map/ppermute | solution.py:25
  33.6 0.5 fusion.11
  34.1 12.8 %collective-permute-done.2 = bf16[8,128,128]{2,1,0:T(8,128)(2,1)S(1)} collective-permute-done((bf16[8,128,128]{2,1,0:T(8,128)(2,1)S(1)}, bf16[8,128,128]{2,1,0:T(8,128)(2,1)S(1)}, u32[]{:S(2)}, u32[]{:S(2)}) %collective-permute-start.2) | collective-permute-done | bytes 262176 | tf_op jit(solution)/shard_map/ppermute | solution.py:25
  46.9 0.0 copy-done.2
  46.9 2.4 %multiply_reduce_fusion = (f32[2,256]{1,0:T(2,128)S(1)}, f32[2,256,8,128]{1,3,2,0:T(8,128)}) fusion(bf16[2,256,8,128]{3,2,1,0:T(8,128)(2,1)S(1)} %bitcast.96, bf16[8,128,128]{2,1,0:T(8,128)(2,1)S(1)} %collective-permute-done.2, f32[2,256,8]{1,2,0:T(8,128)S(1)} %get-tuple-element.6, f32[8,128,2,256]{3,1,0,2:T(8,128)S(1)} %fusion.11, ...), kind=kOutput, calls=%fused_computation.12 | convolution fusion | flops 139460096 | bytes 10815488 | tf_op jit(solution)/shard_map/lwnx,nxq->lwnq/dot_general | solution.py:89
  49.3 5.2 %all-gather = f32[4,1,512]{2,1,0:T(1,128)S(1)} all-gather(f32[1,1,512]{2,1,0:T(1,128)S(1)} %reshape.68), channel_id=1, replica_groups=mesh['seq'=8,'head'=4] {'head'}, dimensions={0}, use_global_device_ids=true | all-gather | bytes 10240 | tf_op jit(solution)/shard_map/all_gather | solution.py:94
  54.5 0.0 copy-start.6
  54.5 2.1 %copy.47 = f32[2,256,8,128]{3,2,1,0:T(8,128)S(1)} copy(f32[2,256,8,128]{1,3,2,0:T(8,128)} %get-tuple-element.10) | data formatting | bytes 4194304 | tf_op jit(solution)/shard_map/add | solution.py:92
  56.7 0.0 copy-done.6
  56.7 1.4 %fusion.1 = bf16[512,1024]{1,0:T(8,128)(2,1)} fusion(f32[64,8,8,128]{3,2,1,0:T(8,128)S(1)} %bitcast.97, f32[1024]{0:T(1024)S(1)} %copy-done.6, f32[512]{0:T(512)S(1)} %add_rsqrt_fusion), kind=kLoop, calls=%fused_computation.3 | loop fusion | flops 1572864 | bytes 3151872 | tf_op jit(solution)/shard_map/convert_element_type | solution.py:99
  (7 shorter events, 0.1 us)
Async XLA Ops:
  0.0 2.3 %copy-start.3 = (bf16[512,1024]{1,0:T(8,128)(2,1)S(1)}, bf16[512,1024]{1,0:T(8,128)(2,1)}, u32[]{:S(2)}) copy-start(bf16[512,1024]{1,0:T(8,128)(2,1)} %param.7) | copy-start | bytes 3145732
  2.3 1.0 %copy-start = (bf16[2,256,8,128]{1,3,2,0:T(8,128)(2,1)}, bf16[2,256,8,128]{1,3,2,0:T(8,128)(2,1)S(1)}, u32[]{:S(2)}) copy-start(bf16[2,256,8,128]{1,3,2,0:T(8,128)(2,1)S(1)} %copy.37) | copy-start | bytes 3145732
  2.6 1.5 %copy-start.1 = (bf16[64,8,8,128]{3,2,1,0:T(8,128)(2,1)}, bf16[64,8,8,128]{3,2,1,0:T(8,128)(2,1)S(1)}, u32[]{:S(2)}) copy-start(bf16[64,8,8,128]{3,2,1,0:T(8,128)(2,1)S(1)} %copy.58) | copy-start | bytes 3145732
  2.6 3.1 %copy-start.5 = (f32[5,8,512]{2,1,0:T(8,128)S(1)}, f32[5,8,512]{2,1,0:T(8,128)}, u32[]{:S(2)}) copy-start(f32[5,8,512]{2,1,0:T(8,128)} %param.8) | copy-start | bytes 245764
  2.6 3.1 %copy-start.4 = (bf16[512,1024]{1,0:T(8,128)(2,1)S(1)}, bf16[512,1024]{1,0:T(8,128)(2,1)}, u32[]{:S(2)}) copy-start(bf16[512,1024]{1,0:T(8,128)(2,1)} %param.5) | copy-start | bytes 3145732
  4.1 14.0 %collective-permute-start = (f32[8,128,128]{2,1,0:T(8,128)}, f32[8,128,128]{2,1,0:T(8,128)}, u32[]{:S(2)}, u32[]{:S(2)}) collective-permute-start(f32[8,128,128]{2,1,0:T(8,128)} %fusion.17), channel_id=1, source_target_pairs={{0,4},{4,0},{8,12},{12,8},{16,20},{20,16},{24,28},{28,24},{1,5},{5... | collective-permute-start | bytes 1572872 | tf_op jit(solution)/shard_map/ppermute | solution.py:19
  19.2 12.9 %collective-permute-start.1 = (f32[8,128,128]{2,1,0:T(8,128)S(1)}, f32[8,128,128]{2,1,0:T(8,128)S(1)}, u32[]{:S(2)}, u32[]{:S(2)}) collective-permute-start(f32[8,128,128]{2,1,0:T(8,128)S(1)} %fusion.34), channel_id=1, source_target_pairs={{0,8},{8,0},{4,12},{12,4},{16,24},{24,16},{20,28},{28,20},{1,9},{9... | collective-permute-start | bytes 1572872 | tf_op jit(solution)/shard_map/ppermute | solution.py:19
  32.1 14.8 %copy-start.2 = (f32[2,8,256,128]{2,3,1,0:T(8,128)S(1)}, f32[2,8,256,128]{2,3,1,0:T(8,128)}, u32[]{:S(2)}) copy-start(f32[2,8,256,128]{2,3,1,0:T(8,128)} %fusion.5) | copy-start | bytes 6291460
  32.1 14.8 %collective-permute-start.2 = (bf16[8,128,128]{2,1,0:T(8,128)(2,1)S(1)}, bf16[8,128,128]{2,1,0:T(8,128)(2,1)S(1)}, u32[]{:S(2)}, u32[]{:S(2)}) collective-permute-start(bf16[8,128,128]{2,1,0:T(8,128)(2,1)S(1)} %add_convert_fusion), channel_id=1, source_target_pairs={{0,16},{4,20},{8,24},{12,28},{1,17},{5,21},{9,25},{13,29},{2,18},{... | collective-permute-start | bytes 786440 | tf_op jit(solution)/shard_map/ppermute | solution.py:25
  54.5 2.1 %copy-start.6 = (f32[1024]{0:T(1024)S(1)}, f32[1024]{0:T(1024)}, u32[]{:S(2)}) copy-start(f32[1024]{0:T(1024)} %param.9) | copy-start | bytes 12292
